TPU v7x, 32 devices: a whole 2x2x4 slice. The times are simulated.
32 devices in a mesh: seq: 16 (over z, y, x), chan: 2 (over core).
Axes of the slice: x: 2, y: 2, z: 4, core: 2. Of those that a mesh axis runs over, the one named last changes fastest.
Arguments:
- inputs: float32 [256, 8192], P('chan', 'seq'), may hold values from -6 to 6
- value_weight: float32 [256, 256], P(None, 'chan'), may hold values from -0.375 to 0.375
- query_weight: float32 [256, 256], P(None, 'chan'), may hold values from -0.375 to 0.375
- filters: float32 [256, 8192], P('chan', 'seq'), may hold values from -1 to 1
- grad_out: float32 [256, 8192], P('chan', 'seq'), may hold values from -6 to 6
Outputs:
- input_grad: float32 [256, 8192], P('chan', 'seq')
- filter_grad: float32 [256, 8192], P('chan', 'seq')
- value_gradient: float32 [256, 256], P(None, 'chan')
- query_gradient: float32 [256, 256], P(None, 'chan')
All inputs are finite; a program needn't handle non-finite values.
Results may differ from a plain program's by a relative error of at most 0.00018.
Values sent between devices are 32-bit elements; how exact they have to be, the bound alone decides.
A program may use at most 64 MiB of HBM per device.

v0:
```python
import functools
import math

import jax
import jax.numpy as jnp
import numpy as np
from jax import lax
from jax.experimental import pallas as pl
from jax.experimental.pallas import tpu as pltpu
from jax.sharding import PartitionSpec as P

BLK = 64
LANES = 128
GROUP = 8


HIGHEST = lax.Precision.HIGHEST


def complex_table(row_count, col_count, period, direction):
    row_iota = lax.broadcasted_iota(jnp.int32, (row_count, col_count), 0)
    col_iota = lax.broadcasted_iota(jnp.int32, (row_count, col_count), 1)
    rotation = 2.0 * math.pi / period * (row_iota * col_iota % period).astype(jnp.float32)
    cosine = jnp.cos(rotation)
    sine_part = direction * jnp.sin(rotation)
    upper_rows = jnp.stack([cosine, sine_part], axis=1)
    lower_rows = jnp.stack([-sine_part, cosine], axis=1)
    return jnp.stack([upper_rows, lower_rows], axis=0)


def rotate(columns, cosine, sine_part):
    return jnp.stack(
        [columns[0] * cosine - columns[1] * sine_part, columns[0] * sine_part + columns[1] * cosine]
    )


def multiply(first_spec, second_spec, conjugate):
    imag_first = -first_spec[1] if conjugate else first_spec[1]
    return jnp.stack(
        [
            first_spec[0] * second_spec[0] - imag_first * second_spec[1],
            first_spec[0] * second_spec[1] + imag_first * second_spec[0],
        ]
    )


def block_angles(block_size, inner_size, seq_rows, direction):
    outer_iota = lax.broadcasted_iota(jnp.int32, (block_size, inner_size), 0)
    inner_iota = lax.broadcasted_iota(jnp.int32, (block_size, inner_size), 1)
    rotation = (
        direction
        * 2.0
        * math.pi
        / seq_rows
        * (outer_iota * inner_iota % seq_rows).astype(jnp.float32)
    )
    return (jnp.cos(rotation)[:, :, None], jnp.sin(rotation)[:, :, None])


def local_forward(columns, block_size):
    seq_rows = columns.shape[1]
    item_width = columns.shape[2]
    inner_size = seq_rows // block_size
    shaped = columns.reshape(2, block_size, inner_size, item_width)
    first_pass = jnp.einsum(
        "xabz,xayk->ykbz",
        shaped,
        complex_table(block_size, block_size, block_size, -1.0),
        precision=HIGHEST,
    )
    cosine, sine_part = block_angles(block_size, inner_size, seq_rows, -1.0)
    rotated = rotate(first_pass, cosine, sine_part)
    second = jnp.einsum(
        "ykbz,ybwm->wkmz",
        rotated,
        complex_table(inner_size, inner_size, inner_size, -1.0),
        precision=HIGHEST,
    )
    return second.reshape(2, seq_rows, item_width)


def local_inverse(columns, block_size):
    seq_rows = columns.shape[1]
    item_width = columns.shape[2]
    inner_size = seq_rows // block_size
    shaped = columns.reshape(2, block_size, inner_size, item_width)
    first_pass = jnp.einsum(
        "xkmz,xmyb->ykbz",
        shaped,
        complex_table(inner_size, inner_size, inner_size, 1.0),
        precision=HIGHEST,
    )
    cosine, sine_part = block_angles(block_size, inner_size, seq_rows, 1.0)
    rotated = rotate(first_pass, cosine, sine_part)
    second = jnp.einsum(
        "xkbz,xkya->yabz",
        rotated,
        complex_table(block_size, block_size, block_size, 1.0),
        precision=HIGHEST,
    )
    return second.reshape(2, seq_rows, item_width) * (1.0 / seq_rows)


def cross_transform(columns, dft_table):
    seq_rows = columns.shape[1]
    item_width = columns.shape[2]
    shaped = columns.reshape(2, 1, seq_rows, item_width)
    transformed = jnp.einsum(
        "xpjz,xpyk->ykjz",
        lax.all_to_all(shaped, "seq", split_axis=2, concat_axis=1, tiled=True),
        dft_table,
        precision=HIGHEST,
    )
    result = lax.all_to_all(transformed, "seq", split_axis=1, concat_axis=2, tiled=True)
    return result.reshape(2, seq_rows, item_width)


def shard_twiddle(columns, frequency, seq_length, direction):
    seq_rows = columns.shape[1]
    local_pos = jnp.arange(seq_rows, dtype=jnp.int32)
    rotation = (
        direction
        * 2.0
        * math.pi
        / seq_length
        * (local_pos * frequency % seq_length).astype(jnp.float32)
    )
    return rotate(columns, jnp.cos(rotation)[:, None], jnp.sin(rotation)[:, None])


def forward(columns, shard_index, devices, block_size):
    seq_length = columns.shape[1] * devices
    columns = cross_transform(columns, complex_table(devices, devices, devices, -1.0))
    columns = shard_twiddle(columns, shard_index, seq_length, -1.0)
    return local_forward(columns, block_size)


def inverse(columns, shard_index, devices, block_size):
    seq_length = columns.shape[1] * devices
    columns = local_inverse(columns, block_size)
    columns = shard_twiddle(columns, shard_index, seq_length, 1.0)
    columns = cross_transform(
        columns, complex_table(devices, devices, devices, 1.0) * (1.0 / devices)
    )
    return columns


def per_device(inputs, value_weight, query_weight, filters, grad_out):
    channel_count = filters.shape[0]
    seq_rows = filters.shape[1]
    devices = lax.axis_size("seq")
    shard_index = lax.axis_index("seq")
    seq_length = seq_rows * devices
    grad_scale = 1.0 / math.sqrt(seq_length)
    all_inputs = lax.all_gather(inputs, "chan", axis=0, tiled=True)
    projected = jnp.einsum("cd,ct->dt", value_weight, all_inputs, precision=HIGHEST)
    query_proj = jnp.einsum("cd,ct->dt", query_weight, all_inputs, precision=HIGHEST)
    gated_grad = grad_out * query_proj
    signals = jnp.stack([projected, filters, gated_grad])
    position = shard_index * seq_rows + jnp.arange(seq_rows, dtype=jnp.int32)
    twist_angle = 0.5 * math.pi / seq_length * position.astype(jnp.float32)
    cosine = jnp.cos(twist_angle)
    sine_part = jnp.sin(twist_angle)
    twisted = jnp.stack([signals * cosine, -signals * sine_part])
    columns = jnp.transpose(twisted, (0, 3, 1, 2)).reshape(2, seq_rows, 3 * channel_count)
    spectra = forward(columns, shard_index, devices, BLK).reshape(2, seq_rows, 3, channel_count)
    value_spec = spectra[:, :, 0]
    filter_spec = spectra[:, :, 1]
    grad_spec = spectra[:, :, 2]
    products = jnp.stack(
        [
            multiply(filter_spec, value_spec, False),
            multiply(filter_spec, grad_spec, True),
            multiply(value_spec, grad_spec, True),
        ],
        axis=2,
    )
    restored = inverse(
        products.reshape(2, seq_rows, 3 * channel_count), shard_index, devices, BLK
    ).reshape(2, seq_rows, 3, channel_count)
    combined = restored[0] * cosine[:, None, None] - restored[1] * sine_part[:, None, None]
    combined = jnp.transpose(combined, (1, 2, 0))
    convolved = combined[0]
    grad_value = combined[1]
    filter_grad = combined[2] * grad_scale
    grad_query = grad_out * convolved
    input_grad = lax.psum_scatter(
        jnp.dot(value_weight, grad_value, precision=HIGHEST, preferred_element_type=jnp.float32)
        + jnp.dot(query_weight, grad_query, precision=HIGHEST, preferred_element_type=jnp.float32),
        "chan",
        scatter_dimension=0,
        tiled=True,
    )
    partial_value = jnp.einsum("ct,dt->cd", all_inputs, grad_value, precision=HIGHEST) * grad_scale
    partial_query = jnp.einsum("ct,dt->cd", all_inputs, grad_query, precision=HIGHEST) * grad_scale
    value_gradient, query_gradient = lax.psum((partial_value, partial_query), "seq")
    return (input_grad, filter_grad, value_gradient, query_gradient)


NN = (((1,), (0,)), ((), ()))
NT = (((1,), (1,)), ((), ()))


def split_table(table):
    high = table.astype(jnp.bfloat16)
    low = (table - high.astype(np.float32)).astype(jnp.bfloat16)
    return high, low


@functools.lru_cache(maxsize=None)
def transform_tables(seq_length):
    outer = seq_length // LANES
    k = np.arange(outer, dtype=np.float64)
    a = np.arange(outer, dtype=np.float64)
    b = np.arange(LANES, dtype=np.float64)
    phase = 2 * np.pi * np.outer(4 * k + 1, a) % (2 * np.pi * 4 * outer) / (4 * outer)
    small = np.concatenate([np.cos(phase), -np.sin(phase)], axis=0)
    wide = np.repeat(small, GROUP, axis=0).astype(np.float32)
    tall = (np.repeat(small.T, GROUP, axis=0) / seq_length).astype(np.float32)
    angle = 2 * np.pi * np.repeat(np.outer(4 * k + 1, b), GROUP, axis=0) / (4 * seq_length)
    turn = np.stack([np.cos(angle), np.sin(angle)]).astype(np.float32)
    inner = 2 * np.pi * (np.outer(b, b) % LANES) / LANES
    c, s = np.cos(inner), np.sin(inner)
    ahead = np.block([[c, -s], [s, c]]).astype(np.float32)
    back = np.block([[c, s], [-s, c]]).astype(np.float32)
    return (
        *split_table(wide),
        *split_table(tall),
        *split_table(ahead),
        *split_table(back),
        turn,
    )


def split(x):
    high = x.astype(jnp.bfloat16)
    return high, (x - high.astype(jnp.float32)).astype(jnp.bfloat16)


def dot3(first, second, dims=NN):
    def dot(x, y):
        return lax.dot_general(x, y, dims, preferred_element_type=jnp.float32)

    return dot(first[0], second[0]) + (dot(first[0], second[1]) + dot(first[1], second[0]))


def spread(small_ref, out_ref):
    rows, cols = out_ref.shape
    inner = small_ref.shape[1]
    pick = lax.broadcasted_iota(jnp.int32, (inner, cols), 1) // GROUP
    own = lax.broadcasted_iota(jnp.int32, (inner, cols), 0)
    picks = jnp.where(pick == own, 1.0, 0.0).astype(jnp.bfloat16)
    row_lane = lax.broadcasted_iota(jnp.int32, (rows, cols), 0) % GROUP
    col_lane = lax.broadcasted_iota(jnp.int32, (rows, cols), 1) % GROUP
    full = lax.dot_general(small_ref[...], picks, NN, preferred_element_type=jnp.float32)
    out_ref[...] = jnp.where(row_lane == col_lane, full, 0.0).astype(jnp.bfloat16)


def fused_kernel(devices, scale, *refs):
    x_hbm, vw_hbm, qw_hbm, f_hbm, g_hbm = refs[:5]
    table_hbm = refs[5:14]
    ig_out, fg_out, vg_out, qg_out = refs[14:18]
    x_ref, vw_ref, qw_ref, g_ref = refs[18:22]
    small_refs = refs[22:26]
    ahead_h, ahead_l, back_h, back_l, turn_ref = refs[26:31]
    wide_h, wide_l, tall_h, tall_l = refs[31:35]
    other_x, send_sig, in_sig, spec, out_sig, ret_sig, part, scat, red, gath = refs[35:45]
    ig_send, ig_recv, ssem, rsem, csend, crecv, lsem = refs[45:]
    me = lax.axis_index("seq")
    chan = lax.axis_index("chan")
    half, width = x_ref.shape
    pieces = width // LANES
    inner = 1 << (devices.bit_length() - 1) // 2
    outer = devices // inner
    rows = 2 * half // inner
    me_inner, me_outer = me % inner, me // inner

    def peer_of(i):
        peer, bit = me, 1
        while bit < devices:
            peer = peer + (i // bit) % 2 * (1 - 2 * (me // bit % 2)) * bit
            bit *= 2
        return peer

    barrier = pltpu.get_barrier_semaphore()

    def greet(i, carry):
        pl.semaphore_signal(
            barrier,
            inc=1,
            device_id={"seq": peer_of(devices - i)},
            device_id_type=pl.DeviceIdType.MESH,
        )
        return carry

    lax.fori_loop(1, devices, greet, 0)
    pl.semaphore_signal(
        barrier, inc=1, device_id={"chan": 1 - chan}, device_id_type=pl.DeviceIdType.MESH
    )

    loads = [
        pltpu.make_async_copy(src, dst, lsem.at[at])
        for at, (src, dst) in enumerate(
            zip(
                (x_hbm, vw_hbm, qw_hbm, g_hbm, *table_hbm),
                (x_ref, vw_ref, qw_ref, g_ref, *small_refs)
                + (ahead_h, ahead_l, back_h, back_l, turn_ref),
            )
        )
    ]
    for load in loads:
        load.start()
    own_f = pl.ds(pl.multiple_of(me * GROUP, GROUP), GROUP)
    keep_f = pltpu.make_async_copy(f_hbm.at[own_f, :], in_sig.at[0, me], lsem.at[len(loads)])
    keep_f.start()
    for load in loads[:3]:
        load.wait()

    own_rows = pl.ds(pl.multiple_of(chan * half, half), half)
    other_rows = pl.ds(pl.multiple_of((1 - chan) * half, half), half)
    own_x = split(x_ref[...])
    partial_value = dot3(split(vw_ref[own_rows, :].T), own_x)
    partial_query = dot3(split(qw_ref[own_rows, :].T), own_x)

    pl.semaphore_wait(barrier, devices)

    def exchange(index, src, dst):
        return pltpu.make_async_remote_copy(
            src_ref=src,
            dst_ref=dst,
            send_sem=csend.at[index],
            recv_sem=crecv.at[index],
            device_id={"chan": 1 - chan},
            device_id_type=pl.DeviceIdType.MESH,
        )

    def each(slot, src_of, dst_of, what, count=devices, stride=1):
        def step(i, carry):
            index = (count - i) * stride
            peer = peer_of(index)
            copy = pltpu.make_async_remote_copy(
                src_ref=src_of(peer),
                dst_ref=dst_of(),
                send_sem=ssem.at[slot, index],
                recv_sem=rsem.at[slot, index],
                device_id={"seq": peer},
                device_id_type=pl.DeviceIdType.MESH,
            )
            getattr(copy, what)()
            return carry

        lax.fori_loop(1, count, step, 0)

    def group_rows(peer, count):
        return pl.ds(pl.multiple_of(peer * count, count), count)

    def out_way(slot, what):
        src = f_hbm if slot == 0 else send_sig.at[slot - 1]
        each(slot, lambda p: src.at[group_rows(p, GROUP), :], lambda: in_sig.at[slot, me], what)

    def back_way(slot, what):
        each(
            3 + slot,
            lambda p: out_sig.at[slot, p],
            lambda: ret_sig.at[slot, group_rows(me, GROUP), :],
            what,
        )

    def scatter(slot, what):
        each(
            6 + slot,
            lambda p: part.at[slot, group_rows(p % inner, rows), :],
            lambda: scat.at[slot, me_inner],
            what,
            inner,
        )

    def swap(slot, what):
        each(
            8 + slot,
            lambda p: red.at[slot, me_outer],
            lambda: red.at[slot, me_outer],
            what,
            outer,
            inner,
        )

    def gather(slot, what):
        each(
            10 + slot,
            lambda p: gath.at[slot, group_rows(me_inner, rows), :],
            lambda: gath.at[slot, group_rows(me_inner, rows), :],
            what,
            inner,
        )

    give_x = exchange(0, x_hbm, other_x)
    give_x.start()
    out_way(0, "start")
    give_x.wait()

    far_x = split(other_x[...])
    send_sig[0] = partial_value + dot3(split(vw_ref[other_rows, :].T), far_x)
    out_way(1, "start")
    in_sig[1, me] = send_sig[0, group_rows(me, GROUP), :]
    query_proj = partial_query + dot3(split(qw_ref[other_rows, :].T), far_x)
    loads[3].wait()
    send_sig[1] = g_ref[...] * query_proj
    out_way(2, "start")
    in_sig[2, me] = send_sig[1, group_rows(me, GROUP), :]

    for load in loads[4:]:
        load.wait()
    for small_ref, out_ref in zip(small_refs, (wide_h, wide_l, tall_h, tall_l)):
        spread(small_ref, out_ref)
    keep_f.wait()
    wide = (wide_h[...], wide_l[...])
    tall = (tall_h[...], tall_l[...])
    ahead = (ahead_h[...], ahead_l[...])
    back = (back_h[...], back_l[...])
    cosine = turn_ref[0]
    sine = turn_ref[1]
    count = cosine.shape[0]

    def transform(slot):
        signal = jnp.concatenate(
            [
                in_sig[slot, source, :, piece * LANES : (piece + 1) * LANES]
                for source in range(devices)
                for piece in range(pieces)
            ],
            axis=0,
        )
        first = dot3(wide, split(signal))
        real, imag = first[:count], first[count:]
        turned = jnp.concatenate(
            [real * cosine + imag * sine, imag * cosine - real * sine], axis=1
        )
        spec[slot] = dot3(split(turned), ahead)

    def restore(first, second, conjugate, slot):
        real_a, imag_a = spec[first, :, :LANES], spec[first, :, LANES:]
        real_b, imag_b = spec[second, :, :LANES], spec[second, :, LANES:]
        if conjugate:
            imag_a = -imag_a
        product = jnp.concatenate(
            [real_a * real_b - imag_a * imag_b, real_a * imag_b + imag_a * real_b], axis=1
        )
        inner = dot3(split(product), back)
        real, imag = inner[:, :LANES], inner[:, LANES:]
        turned = jnp.concatenate(
            [real * cosine - imag * sine, imag * cosine + real * sine], axis=0
        )
        signal = dot3(tall, split(turned))
        if slot == 2:
            signal = signal * scale
        for target in range(devices):
            for piece in range(pieces):
                at = (target * pieces + piece) * GROUP
                out_sig[slot, target, :, piece * LANES : (piece + 1) * LANES] = signal[
                    at : at + GROUP
                ]
        back_way(slot, "start")
        ret_sig[slot, group_rows(me, GROUP), :] = out_sig[slot, me]

    out_way(0, "wait_recv")
    transform(0)
    out_way(1, "wait_recv")
    transform(1)
    restore(0, 1, False, 0)
    out_way(2, "wait_recv")
    transform(2)
    restore(0, 2, True, 1)
    restore(1, 2, True, 2)

    def weight_part(slot, grad):
        part[slot, own_rows, :] = dot3(own_x2, grad, NT)
        part[slot, other_rows, :] = dot3(far_x2, grad, NT)
        scatter(slot, "start")
        scat[slot, me_inner] = part[slot, group_rows(me_inner, rows), :]

    own_x2 = split(x_ref[...])
    far_x2 = split(other_x[...])
    back_way(0, "wait_recv")
    grad_query = split(g_ref[...] * ret_sig[0])
    weight_part(0, grad_query)
    near_grad = dot3(split(qw_ref[own_rows, :]), grad_query)
    far_grad = dot3(split(qw_ref[other_rows, :]), grad_query)

    def reduce_inner(slot):
        scatter(slot, "wait_recv")
        total = scat[slot, 0]
        for source in range(1, inner):
            total = total + scat[slot, source]
        red[slot, me_outer] = total
        swap(slot, "start")

    def reduce_outer(slot):
        swap(slot, "wait_recv")
        total = red[slot, 0]
        for source in range(1, outer):
            total = total + red[slot, source]
        gath[slot, group_rows(me_inner, rows), :] = total * scale
        gather(slot, "start")

    reduce_inner(0)
    back_way(1, "wait_recv")
    grad_value = split(ret_sig[1])
    weight_part(1, grad_value)
    ig_send[...] = far_grad + dot3(split(vw_ref[other_rows, :]), grad_value)
    give_ig = exchange(1, ig_send, ig_recv)
    give_ig.start()
    reduce_inner(1)
    near_grad = near_grad + dot3(split(vw_ref[own_rows, :]), grad_value)
    reduce_outer(0)
    give_ig.wait()
    ig_out[...] = near_grad + ig_recv[...]
    reduce_outer(1)
    back_way(2, "wait_recv")
    fg_out[...] = ret_sig[2]
    for slot, out in ((0, qg_out), (1, vg_out)):
        gather(slot, "wait_recv")
        out[...] = gath[slot]
    for slot in range(3):
        out_way(slot, "wait_send")
        back_way(slot, "wait_send")
    for slot in range(2):
        scatter(slot, "wait_send")
        swap(slot, "wait_send")
        gather(slot, "wait_send")


def finish_kernel(*refs):
    stores = [
        pltpu.make_async_copy(source, target, refs[8].at[at])
        for at, (source, target) in enumerate(zip(refs[:4], refs[4:8]))
    ]
    for store in stores:
        store.start()
    for store in stores:
        store.wait()


def fused_device(inputs, value_weight, query_weight, filters, grad_out):
    half, width = inputs.shape
    devices = lax.axis_size("seq")
    seq_length = width * devices
    depth = value_weight.shape[0]
    inner = 1 << (devices.bit_length() - 1) // 2
    outer = devices // inner
    rows = depth // inner
    tables = transform_tables(seq_length)
    count = seq_length // LANES * GROUP
    tables = [jnp.asarray(t) for t in tables]
    hbm = pl.BlockSpec(memory_space=pltpu.HBM)
    vmem = pl.BlockSpec(memory_space=pltpu.VMEM)
    f32, bf16 = jnp.float32, jnp.bfloat16
    outs = (
        jax.ShapeDtypeStruct((half, width), f32),
        jax.ShapeDtypeStruct((half, width), f32),
        jax.ShapeDtypeStruct((depth, half), f32),
        jax.ShapeDtypeStruct((depth, half), f32),
    )
    results = pl.pallas_call(
        functools.partial(fused_kernel, devices, 1.0 / math.sqrt(seq_length)),
        out_shape=tuple(pltpu.VMEM(out.shape, out.dtype) for out in outs),
        in_specs=[hbm] * (5 + len(tables)),
        out_specs=(vmem,) * 4,
        scratch_shapes=[
            pltpu.VMEM((half, width), f32),
            pltpu.VMEM((depth, half), f32),
            pltpu.VMEM((depth, half), f32),
            pltpu.VMEM((half, width), f32),
            *(pltpu.VMEM(t.shape, t.dtype) for t in tables),
            pltpu.VMEM((2 * count, count), bf16),
            pltpu.VMEM((2 * count, count), bf16),
            pltpu.VMEM((count, 2 * count), bf16),
            pltpu.VMEM((count, 2 * count), bf16),
            pltpu.VMEM((half, width), f32),
            pltpu.VMEM((2, half, width), f32),
            pltpu.VMEM((3, devices, GROUP, width), f32),
            pltpu.VMEM((3, count, 2 * LANES), f32),
            pltpu.VMEM((3, devices, GROUP, width), f32),
            pltpu.VMEM((3, half, width), f32),
            pltpu.VMEM((2, depth, half), f32),
            pltpu.VMEM((2, inner, rows, half), f32),
            pltpu.VMEM((2, outer, rows, half), f32),
            pltpu.VMEM((2, depth, half), f32),
            pltpu.VMEM((half, width), f32),
            pltpu.VMEM((half, width), f32),
            pltpu.SemaphoreType.DMA((12, devices)),
            pltpu.SemaphoreType.DMA((12, devices)),
            pltpu.SemaphoreType.DMA((2,)),
            pltpu.SemaphoreType.DMA((2,)),
            pltpu.SemaphoreType.DMA((5 + len(tables),)),
        ],
        compiler_params=pltpu.CompilerParams(
            collective_id=0, has_side_effects=True, vmem_limit_bytes=60 * 1024 * 1024
        ),
    )(inputs, value_weight, query_weight, filters, grad_out, *tables)
    return tuple(
        pl.pallas_call(
            finish_kernel,
            out_shape=outs,
            in_specs=[vmem] * 4,
            out_specs=(hbm,) * 4,
            scratch_shapes=[pltpu.SemaphoreType.DMA((4,))],
        )(*(pltpu.with_memory_space_constraint(r, pltpu.VMEM) for r in results))
    )


def on_device(inputs, value_weight, query_weight, filters, grad_out):
    channel_count, width = filters.shape
    devices = lax.axis_size("seq")
    fits = (
        channel_count == GROUP * devices
        and channel_count == inputs.shape[0]
        and lax.axis_size("chan") == 2
        and width % LANES == 0
        and channel_count % LANES == 0
        and devices & (devices - 1) == 0
        and value_weight.shape[0] % (GROUP * devices) == 0
    )
    body = fused_device if fits else per_device
    return body(inputs, value_weight, query_weight, filters, grad_out)


def solution(mesh):
    return jax.shard_map(
        on_device,
        mesh=mesh,
        in_specs=(
            P("chan", "seq"),
            P(None, "chan"),
            P(None, "chan"),
            P("chan", "seq"),
            P("chan", "seq"),
        ),
        out_specs=(P("chan", "seq"), P("chan", "seq"), P(None, "chan"), P(None, "chan")),
        check_vma=False,
    )
```

profile of v0, /device:TPU:0, one launch (start us, length us, event | category | flops | bytes accessed | tf_op | source)
XLA Modules:
  0.0 59.4 jit_solution(12985259055940559595)
XLA Ops:
  0.6 57.8 %shard_map.165 = (f32[128,512]{1,0:T(8,128)S(1)}, f32[128,512]{1,0:T(8,128)S(1)}, f32[256,128]{1,0:T(8,128)S(1)}, f32[256,128]{1,0:T(8,128)S(1)}) custom-call(f32[128,512]{1,0:T(8,128)} %refs_0_.1, f32[256,128]{1,0:T(8,128)} %refs_1_.1, f32[256,128]{1,0:T(8,128)} %refs_2_.1, f32[128,512]{1,0:T(8,128)} %refs_3_.1, f32[128,512]{1,0:T(8,128)} %refs_4_.1, ...), custom_call_target="tpu_custom_call" | custom-call | tf_op jit(solution)/shard_map/pallas_call | solution.py:564
  58.5 0.9 %shard_map.166 = (f32[128,512]{1,0:T(8,128)}, f32[128,512]{1,0:T(8,128)}, f32[256,128]{1,0:T(8,128)}, f32[256,128]{1,0:T(8,128)}) custom-call(f32[128,512]{1,0:T(8,128)S(1)} %get-tuple-element.8.refs_0_, f32[128,512]{1,0:T(8,128)S(1)} %get-tuple-element.9.refs_1_, f32[256,128]{1,0:T(8,128)S(1)} %get-tuple-element.10.refs_2_, ...), custom_call_target="tpu_custom_call" | custom-call | tf_op jit(solution)/shard_map/pallas_call | solution.py:602
where the time goes:
time: 59.5 us; the launch traced here: 59.4 us
  Pallas kernels  58.8 us (99%)
  between operations  0.64 us (1%)
    pallas_call x1, Pallas kernels, fused_device(): pl.pallas_call(functools.partial(fused_kernel, devices, 1.0 / math.sqrt(s...  57.8 us

commit v1 on v0

--- a/solution.py
+++ b/solution.py
@@ -313,15 +313,6 @@
     own_f = pl.ds(pl.multiple_of(me * GROUP, GROUP), GROUP)
     keep_f = pltpu.make_async_copy(f_hbm.at[own_f, :], in_sig.at[0, me], lsem.at[len(loads)])
     keep_f.start()
-    for load in loads[:3]:
-        load.wait()
-
-    own_rows = pl.ds(pl.multiple_of(chan * half, half), half)
-    other_rows = pl.ds(pl.multiple_of((1 - chan) * half, half), half)
-    own_x = split(x_ref[...])
-    partial_value = dot3(split(vw_ref[own_rows, :].T), own_x)
-    partial_query = dot3(split(qw_ref[own_rows, :].T), own_x)
-
     pl.semaphore_wait(barrier, devices)
 
     def exchange(index, src, dst):
@@ -334,69 +325,93 @@
             device_id_type=pl.DeviceIdType.MESH,
         )
 
-    def each(slot, src_of, dst_of, what, count=devices, stride=1):
+    def send_each(slot, src_of, dst, count=devices, stride=1):
         def step(i, carry):
-            index = (count - i) * stride
-            peer = peer_of(index)
-            copy = pltpu.make_async_remote_copy(
+            peer = peer_of((count - i) * stride)
+            pltpu.make_async_remote_copy(
                 src_ref=src_of(peer),
-                dst_ref=dst_of(),
-                send_sem=ssem.at[slot, index],
-                recv_sem=rsem.at[slot, index],
+                dst_ref=dst,
+                send_sem=ssem.at[slot],
+                recv_sem=rsem.at[slot],
                 device_id={"seq": peer},
                 device_id_type=pl.DeviceIdType.MESH,
-            )
-            getattr(copy, what)()
+            ).start()
             return carry
 
         lax.fori_loop(1, count, step, 0)
+
+    def drain(slot, ref, what):
+        copy = pltpu.make_async_remote_copy(
+            src_ref=ref,
+            dst_ref=ref,
+            send_sem=ssem.at[slot],
+            recv_sem=rsem.at[slot],
+            device_id={"seq": peer_of(1)},
+            device_id_type=pl.DeviceIdType.MESH,
+        )
+        getattr(copy, what)()
 
     def group_rows(peer, count):
         return pl.ds(pl.multiple_of(peer * count, count), count)
 
     def out_way(slot, what):
-        src = f_hbm if slot == 0 else send_sig.at[slot - 1]
-        each(slot, lambda p: src.at[group_rows(p, GROUP), :], lambda: in_sig.at[slot, me], what)
+        if what == "start":
+            src = f_hbm if slot == 0 else send_sig.at[slot - 1]
+            send_each(slot, lambda p: src.at[group_rows(p, GROUP), :], in_sig.at[slot, me])
+        else:
+            drain(slot, in_sig.at[slot, pl.ds(0, devices - 1)], what)
 
     def back_way(slot, what):
-        each(
-            3 + slot,
-            lambda p: out_sig.at[slot, p],
-            lambda: ret_sig.at[slot, group_rows(me, GROUP), :],
-            what,
-        )
+        if what == "start":
+            send_each(
+                3 + slot,
+                lambda p: out_sig.at[slot, p],
+                ret_sig.at[slot, group_rows(me, GROUP), :],
+            )
+        else:
+            drain(3 + slot, out_sig.at[slot, pl.ds(0, devices - 1)], what)
 
     def scatter(slot, what):
-        each(
-            6 + slot,
-            lambda p: part.at[slot, group_rows(p % inner, rows), :],
-            lambda: scat.at[slot, me_inner],
-            what,
-            inner,
-        )
+        if what == "start":
+            send_each(
+                6 + slot,
+                lambda p: part.at[slot, group_rows(p % inner, rows), :],
+                scat.at[slot, me_inner],
+                inner,
+            )
+        else:
+            drain(6 + slot, scat.at[slot, pl.ds(0, inner - 1)], what)
 
     def swap(slot, what):
-        each(
-            8 + slot,
-            lambda p: red.at[slot, me_outer],
-            lambda: red.at[slot, me_outer],
-            what,
-            outer,
-            inner,
-        )
+        if what == "start":
+            send_each(
+                8 + slot,
+                lambda p: red.at[slot, me_outer],
+                red.at[slot, me_outer],
+                outer,
+                inner,
+            )
+        else:
+            drain(8 + slot, red.at[slot, pl.ds(0, outer - 1)], what)
 
     def gather(slot, what):
-        each(
-            10 + slot,
-            lambda p: gath.at[slot, group_rows(me_inner, rows), :],
-            lambda: gath.at[slot, group_rows(me_inner, rows), :],
-            what,
-            inner,
-        )
+        mine = gath.at[slot, group_rows(me_inner, rows), :]
+        if what == "start":
+            send_each(10 + slot, lambda p: mine, mine, inner)
+        else:
+            drain(10 + slot, gath.at[slot, pl.ds(0, (inner - 1) * rows), :], what)
 
     give_x = exchange(0, x_hbm, other_x)
     give_x.start()
     out_way(0, "start")
+
+    for load in loads[:3]:
+        load.wait()
+    own_rows = pl.ds(pl.multiple_of(chan * half, half), half)
+    other_rows = pl.ds(pl.multiple_of((1 - chan) * half, half), half)
+    own_x = split(x_ref[...])
+    partial_value = dot3(split(vw_ref[own_rows, :].T), own_x)
+    partial_query = dot3(split(qw_ref[own_rows, :].T), own_x)
     give_x.wait()
 
     far_x = split(other_x[...])
@@ -588,8 +603,8 @@
             pltpu.VMEM((2, depth, half), f32),
             pltpu.VMEM((half, width), f32),
             pltpu.VMEM((half, width), f32),
-            pltpu.SemaphoreType.DMA((12, devices)),
-            pltpu.SemaphoreType.DMA((12, devices)),
+            pltpu.SemaphoreType.DMA((12,)),
+            pltpu.SemaphoreType.DMA((12,)),
             pltpu.SemaphoreType.DMA((2,)),
             pltpu.SemaphoreType.DMA((2,)),
             pltpu.SemaphoreType.DMA((5 + len(tables),)),

time: 59.5 us -> 55.6 us (0.934)
  Pallas kernels: 58.8 us -> 54.8 us
    pallas_call x1, Pallas kernels: 57.8 us -> 53.8 us  [fused_device(): pl.pallas_call(functools.partial(fused_kernel, devices, 1.0 / math.sqrt(s...]
where the time goes in v1:
time: 55.6 us; the launch traced here: 55.4 us
  Pallas kernels  54.8 us (99%)
  between operations  0.64 us (1%)
    pallas_call x1, Pallas kernels, fused_device(): pl.pallas_call(functools.partial(fused_kernel, devices, 1.0 / math.sqrt(s...  53.8 us

profile of v1, /device:TPU:0, one launch (start us, length us, event | category | flops | bytes accessed | tf_op | source)
XLA Modules:
  0.0 55.4 jit_solution(2420271442945337814)
XLA Ops:
  0.6 53.8 %shard_map.165 = (f32[128,512]{1,0:T(8,128)S(1)}, f32[128,512]{1,0:T(8,128)S(1)}, f32[256,128]{1,0:T(8,128)S(1)}, f32[256,128]{1,0:T(8,128)S(1)}) custom-call(f32[128,512]{1,0:T(8,128)} %refs_0_.1, f32[256,128]{1,0:T(8,128)} %refs_1_.1, f32[256,128]{1,0:T(8,128)} %refs_2_.1, f32[128,512]{1,0:T(8,128)} %refs_3_.1, f32[128,512]{1,0:T(8,128)} %refs_4_.1, ...), custom_call_target="tpu_custom_call" | custom-call | tf_op jit(solution)/shard_map/pallas_call | solution.py:579
  54.5 0.9 %shard_map.166 = (f32[128,512]{1,0:T(8,128)}, f32[128,512]{1,0:T(8,128)}, f32[256,128]{1,0:T(8,128)}, f32[256,128]{1,0:T(8,128)}) custom-call(f32[128,512]{1,0:T(8,128)S(1)} %get-tuple-element.8.refs_0_, f32[128,512]{1,0:T(8,128)S(1)} %get-tuple-element.9.refs_1_, f32[256,128]{1,0:T(8,128)S(1)} %get-tuple-element.10.refs_2_, ...), custom_call_target="tpu_custom_call" | custom-call | tf_op jit(solution)/shard_map/pallas_call | solution.py:617

commit v2 on v1

--- a/solution.py
+++ b/solution.py
@@ -199,6 +199,7 @@
 
 NN = (((1,), (0,)), ((), ()))
 NT = (((1,), (1,)), ((), ()))
+scope = jax.named_scope
 
 
 def split_table(table):
@@ -215,19 +216,19 @@
     b = np.arange(LANES, dtype=np.float64)
     phase = 2 * np.pi * np.outer(4 * k + 1, a) % (2 * np.pi * 4 * outer) / (4 * outer)
     small = np.concatenate([np.cos(phase), -np.sin(phase)], axis=0)
-    wide = np.repeat(small, GROUP, axis=0).astype(np.float32)
-    tall = (np.repeat(small.T, GROUP, axis=0) / seq_length).astype(np.float32)
-    angle = 2 * np.pi * np.repeat(np.outer(4 * k + 1, b), GROUP, axis=0) / (4 * seq_length)
+    wide_h, wide_l = split_table(small.astype(np.float32))
+    tall_h, tall_l = split_table((small.T / seq_length).astype(np.float32))
+    angle = 2 * np.pi * np.outer(4 * k + 1, b) / (4 * seq_length)
     turn = np.stack([np.cos(angle), np.sin(angle)]).astype(np.float32)
     inner = 2 * np.pi * (np.outer(b, b) % LANES) / LANES
     c, s = np.cos(inner), np.sin(inner)
-    ahead = np.block([[c, -s], [s, c]]).astype(np.float32)
-    back = np.block([[c, s], [-s, c]]).astype(np.float32)
+    ahead_h, ahead_l = split_table(np.block([[c, -s], [s, c]]).astype(np.float32))
+    back_h, back_l = split_table(np.block([[c, s], [-s, c]]).astype(np.float32))
     return (
-        *split_table(wide),
-        *split_table(tall),
-        *split_table(ahead),
-        *split_table(back),
+        np.concatenate([wide_h, wide_l, wide_h, wide_l], axis=1),
+        np.concatenate([tall_h, tall_l, tall_h, tall_l], axis=1),
+        np.concatenate([ahead_h, ahead_h, ahead_l], axis=0),
+        np.concatenate([back_h, back_h, back_l], axis=0),
         turn,
     )
 
@@ -244,28 +245,28 @@
     return dot(first[0], second[0]) + (dot(first[0], second[1]) + dot(first[1], second[0]))
 
 
-def spread(small_ref, out_ref):
-    rows, cols = out_ref.shape
-    inner = small_ref.shape[1]
-    pick = lax.broadcasted_iota(jnp.int32, (inner, cols), 1) // GROUP
-    own = lax.broadcasted_iota(jnp.int32, (inner, cols), 0)
-    picks = jnp.where(pick == own, 1.0, 0.0).astype(jnp.bfloat16)
-    row_lane = lax.broadcasted_iota(jnp.int32, (rows, cols), 0) % GROUP
-    col_lane = lax.broadcasted_iota(jnp.int32, (rows, cols), 1) % GROUP
-    full = lax.dot_general(small_ref[...], picks, NN, preferred_element_type=jnp.float32)
-    out_ref[...] = jnp.where(row_lane == col_lane, full, 0.0).astype(jnp.bfloat16)
+def dot(first, second):
+    return lax.dot_general(first, second, NN, preferred_element_type=jnp.float32)
+
+
+def left3(x):
+    high, low = split(x)
+    return jnp.concatenate([high, low, high], axis=1)
+
+
+def right4(x):
+    high, low = split(x)
+    return jnp.concatenate([high, high, low, low], axis=0)
 
 
 def fused_kernel(devices, scale, *refs):
     x_hbm, vw_hbm, qw_hbm, f_hbm, g_hbm = refs[:5]
-    table_hbm = refs[5:14]
-    ig_out, fg_out, vg_out, qg_out = refs[14:18]
-    x_ref, vw_ref, qw_ref, g_ref = refs[18:22]
-    small_refs = refs[22:26]
-    ahead_h, ahead_l, back_h, back_l, turn_ref = refs[26:31]
-    wide_h, wide_l, tall_h, tall_l = refs[31:35]
-    other_x, send_sig, in_sig, spec, out_sig, ret_sig, part, scat, red, gath = refs[35:45]
-    ig_send, ig_recv, ssem, rsem, csend, crecv, lsem = refs[45:]
+    table_hbm = refs[5:10]
+    ig_out, fg_out, vg_out, qg_out = refs[10:14]
+    x_ref, vw_ref, qw_ref, g_ref = refs[14:18]
+    wide_ref, tall_ref, ahead_ref, back_ref, turn_ref = refs[18:23]
+    other_x, f_sig, send_sig, in_sig, spec, out_sig, ret_sig, part, scat, red, gath = refs[23:34]
+    ig_send, ig_recv, ssem, rsem, csend, crecv, lsem = refs[34:]
     me = lax.axis_index("seq")
     chan = lax.axis_index("chan")
     half, width = x_ref.shape
@@ -298,21 +299,30 @@
         barrier, inc=1, device_id={"chan": 1 - chan}, device_id_type=pl.DeviceIdType.MESH
     )
 
+    def lanes(piece):
+        return slice(piece * LANES, (piece + 1) * LANES)
+
     loads = [
         pltpu.make_async_copy(src, dst, lsem.at[at])
         for at, (src, dst) in enumerate(
-            zip(
-                (x_hbm, vw_hbm, qw_hbm, g_hbm, *table_hbm),
-                (x_ref, vw_ref, qw_ref, g_ref, *small_refs)
-                + (ahead_h, ahead_l, back_h, back_l, turn_ref),
-            )
+            [
+                *((f_hbm.at[:, lanes(piece)], f_sig.at[piece]) for piece in range(pieces)),
+                (x_hbm, x_ref),
+                (vw_hbm, vw_ref),
+                (qw_hbm, qw_ref),
+                (g_hbm, g_ref),
+                *zip(table_hbm, (wide_ref, tall_ref, ahead_ref, back_ref, turn_ref)),
+            ]
         )
     ]
     for load in loads:
         load.start()
-    own_f = pl.ds(pl.multiple_of(me * GROUP, GROUP), GROUP)
-    keep_f = pltpu.make_async_copy(f_hbm.at[own_f, :], in_sig.at[0, me], lsem.at[len(loads)])
-    keep_f.start()
+
+    def wait_loads(count):
+        for load in loads[:count]:
+            load.wait()
+        del loads[:count]
+
     pl.semaphore_wait(barrier, devices)
 
     def exchange(index, src, dst):
@@ -356,20 +366,26 @@
 
     def out_way(slot, what):
         if what == "start":
-            src = f_hbm if slot == 0 else send_sig.at[slot - 1]
-            send_each(slot, lambda p: src.at[group_rows(p, GROUP), :], in_sig.at[slot, me])
+            src = f_sig if slot == 0 else send_sig.at[slot - 1]
+            send_each(
+                slot,
+                lambda p: src.at[:, group_rows(p, GROUP), :],
+                in_sig.at[slot, group_rows(me, pieces)],
+            )
+            in_sig[slot, group_rows(me, pieces)] = src[:, group_rows(me, GROUP), :]
         else:
-            drain(slot, in_sig.at[slot, pl.ds(0, devices - 1)], what)
+            drain(slot, in_sig.at[slot, pl.ds(0, (devices - 1) * pieces)], what)
 
     def back_way(slot, what):
         if what == "start":
             send_each(
                 3 + slot,
-                lambda p: out_sig.at[slot, p],
-                ret_sig.at[slot, group_rows(me, GROUP), :],
+                lambda p: out_sig.at[slot, group_rows(p, pieces)],
+                ret_sig.at[slot, :, group_rows(me, GROUP), :],
             )
+            ret_sig[slot, :, group_rows(me, GROUP), :] = out_sig[slot, group_rows(me, pieces)]
         else:
-            drain(3 + slot, out_sig.at[slot, pl.ds(0, devices - 1)], what)
+            drain(3 + slot, out_sig.at[slot, pl.ds(0, (devices - 1) * pieces)], what)
 
     def scatter(slot, what):
         if what == "start":
@@ -403,55 +419,64 @@
 
     give_x = exchange(0, x_hbm, other_x)
     give_x.start()
-    out_way(0, "start")
-
-    for load in loads[:3]:
-        load.wait()
+    with scope("load_f"):
+        wait_loads(pieces)
+    with scope("out0"):
+        out_way(0, "start")
+
+    wait_loads(3)
     own_rows = pl.ds(pl.multiple_of(chan * half, half), half)
     other_rows = pl.ds(pl.multiple_of((1 - chan) * half, half), half)
     own_x = split(x_ref[...])
     partial_value = dot3(split(vw_ref[own_rows, :].T), own_x)
     partial_query = dot3(split(qw_ref[own_rows, :].T), own_x)
-    give_x.wait()
+    with scope("give_x"):
+        give_x.wait()
+
+    def stage(slot, value):
+        for piece in range(pieces):
+            send_sig[slot - 1, piece] = value[:, lanes(piece)]
+        with scope("out"):
+            out_way(slot, "start")
 
     far_x = split(other_x[...])
-    send_sig[0] = partial_value + dot3(split(vw_ref[other_rows, :].T), far_x)
-    out_way(1, "start")
-    in_sig[1, me] = send_sig[0, group_rows(me, GROUP), :]
+    stage(1, partial_value + dot3(split(vw_ref[other_rows, :].T), far_x))
     query_proj = partial_query + dot3(split(qw_ref[other_rows, :].T), far_x)
-    loads[3].wait()
-    send_sig[1] = g_ref[...] * query_proj
-    out_way(2, "start")
-    in_sig[2, me] = send_sig[1, group_rows(me, GROUP), :]
-
-    for load in loads[4:]:
-        load.wait()
-    for small_ref, out_ref in zip(small_refs, (wide_h, wide_l, tall_h, tall_l)):
-        spread(small_ref, out_ref)
-    keep_f.wait()
-    wide = (wide_h[...], wide_l[...])
-    tall = (tall_h[...], tall_l[...])
-    ahead = (ahead_h[...], ahead_l[...])
-    back = (back_h[...], back_l[...])
+    wait_loads(1)
+    stage(2, g_ref[...] * query_proj)
+
+    wait_loads(len(loads))
+    wide = wide_ref[...]
+    tall = tall_ref[...]
+    ahead = ahead_ref[...]
+    back = back_ref[...]
     cosine = turn_ref[0]
     sine = turn_ref[1]
-    count = cosine.shape[0]
+    outer_len = cosine.shape[0]
+
+    def channel_rows(channel):
+        return slice(channel * outer_len, (channel + 1) * outer_len)
+
+    def channel_of(channel):
+        return pl.ds(channel, outer_len, stride=GROUP)
 
     def transform(slot):
-        signal = jnp.concatenate(
-            [
-                in_sig[slot, source, :, piece * LANES : (piece + 1) * LANES]
-                for source in range(devices)
-                for piece in range(pieces)
-            ],
-            axis=0,
-        )
-        first = dot3(wide, split(signal))
-        real, imag = first[:count], first[count:]
-        turned = jnp.concatenate(
-            [real * cosine + imag * sine, imag * cosine - real * sine], axis=1
-        )
-        spec[slot] = dot3(split(turned), ahead)
+        signal = in_sig.at[slot].reshape(outer_len * GROUP, LANES)
+        rows_of = []
+        for pair in range(0, GROUP, 2):
+            columns = jnp.concatenate(
+                [signal[channel_of(channel), :] for channel in (pair, pair + 1)], axis=1
+            )
+            first = dot(wide, right4(columns))
+            for at in range(2):
+                real = first[:outer_len, lanes(at)]
+                imag = first[outer_len:, lanes(at)]
+                rows_of.append(
+                    jnp.concatenate(
+                        [real * cosine + imag * sine, imag * cosine - real * sine], axis=1
+                    )
+                )
+        spec[slot] = dot(left3(jnp.concatenate(rows_of, axis=0)), ahead)
 
     def restore(first, second, conjugate, slot):
         real_a, imag_a = spec[first, :, :LANES], spec[first, :, LANES:]
@@ -461,32 +486,46 @@
         product = jnp.concatenate(
             [real_a * real_b - imag_a * imag_b, real_a * imag_b + imag_a * real_b], axis=1
         )
-        inner = dot3(split(product), back)
-        real, imag = inner[:, :LANES], inner[:, LANES:]
-        turned = jnp.concatenate(
-            [real * cosine - imag * sine, imag * cosine + real * sine], axis=0
-        )
-        signal = dot3(tall, split(turned))
-        if slot == 2:
-            signal = signal * scale
-        for target in range(devices):
-            for piece in range(pieces):
-                at = (target * pieces + piece) * GROUP
-                out_sig[slot, target, :, piece * LANES : (piece + 1) * LANES] = signal[
-                    at : at + GROUP
-                ]
+        inverse = dot(left3(product), back)
+        target = out_sig.at[slot].reshape(outer_len * GROUP, LANES)
+        for pair in range(0, GROUP, 2):
+            columns = []
+            for channel in (pair, pair + 1):
+                real = inverse[channel_rows(channel), :LANES]
+                imag = inverse[channel_rows(channel), LANES:]
+                columns.append(
+                    jnp.concatenate(
+                        [real * cosine - imag * sine, imag * cosine + real * sine], axis=0
+                    )
+                )
+            signal = dot(tall, right4(jnp.concatenate(columns, axis=1)))
+            if slot == 2:
+                signal = signal * scale
+            for at in range(2):
+                target[channel_of(pair + at), :] = signal[:, lanes(at)]
         back_way(slot, "start")
-        ret_sig[slot, group_rows(me, GROUP), :] = out_sig[slot, me]
-
-    out_way(0, "wait_recv")
-    transform(0)
-    out_way(1, "wait_recv")
-    transform(1)
-    restore(0, 1, False, 0)
-    out_way(2, "wait_recv")
-    transform(2)
-    restore(0, 2, True, 1)
-    restore(1, 2, True, 2)
+
+    def returned(slot):
+        return jnp.concatenate([ret_sig[slot, piece] for piece in range(pieces)], axis=1)
+
+    with scope("wait0"):
+        out_way(0, "wait_recv")
+    with scope("t0"):
+        transform(0)
+    with scope("wait1"):
+        out_way(1, "wait_recv")
+    with scope("t1"):
+        transform(1)
+    with scope("r0"):
+        restore(0, 1, False, 0)
+    with scope("wait2"):
+        out_way(2, "wait_recv")
+    with scope("t2"):
+        transform(2)
+    with scope("r1"):
+        restore(0, 2, True, 1)
+    with scope("r2"):
+        restore(1, 2, True, 2)
 
     def weight_part(slot, grad):
         part[slot, own_rows, :] = dot3(own_x2, grad, NT)
@@ -496,14 +535,16 @@
 
     own_x2 = split(x_ref[...])
     far_x2 = split(other_x[...])
-    back_way(0, "wait_recv")
-    grad_query = split(g_ref[...] * ret_sig[0])
+    with scope("back0"):
+        back_way(0, "wait_recv")
+    grad_query = split(g_ref[...] * returned(0))
     weight_part(0, grad_query)
     near_grad = dot3(split(qw_ref[own_rows, :]), grad_query)
     far_grad = dot3(split(qw_ref[other_rows, :]), grad_query)
 
     def reduce_inner(slot):
-        scatter(slot, "wait_recv")
+        with scope(f"scat{slot}"):
+            scatter(slot, "wait_recv")
         total = scat[slot, 0]
         for source in range(1, inner):
             total = total + scat[slot, source]
@@ -511,7 +552,8 @@
         swap(slot, "start")
 
     def reduce_outer(slot):
-        swap(slot, "wait_recv")
+        with scope(f"swap{slot}"):
+            swap(slot, "wait_recv")
         total = red[slot, 0]
         for source in range(1, outer):
             total = total + red[slot, source]
@@ -519,8 +561,9 @@
         gather(slot, "start")
 
     reduce_inner(0)
-    back_way(1, "wait_recv")
-    grad_value = split(ret_sig[1])
+    with scope("back1"):
+        back_way(1, "wait_recv")
+    grad_value = split(returned(1))
     weight_part(1, grad_value)
     ig_send[...] = far_grad + dot3(split(vw_ref[other_rows, :]), grad_value)
     give_ig = exchange(1, ig_send, ig_recv)
@@ -528,21 +571,25 @@
     reduce_inner(1)
     near_grad = near_grad + dot3(split(vw_ref[own_rows, :]), grad_value)
     reduce_outer(0)
-    give_ig.wait()
+    with scope("give_ig"):
+        give_ig.wait()
     ig_out[...] = near_grad + ig_recv[...]
     reduce_outer(1)
-    back_way(2, "wait_recv")
-    fg_out[...] = ret_sig[2]
+    with scope("back2"):
+        back_way(2, "wait_recv")
+    fg_out[...] = returned(2)
     for slot, out in ((0, qg_out), (1, vg_out)):
-        gather(slot, "wait_recv")
+        with scope(f"gather{slot}"):
+            gather(slot, "wait_recv")
         out[...] = gath[slot]
-    for slot in range(3):
-        out_way(slot, "wait_send")
-        back_way(slot, "wait_send")
-    for slot in range(2):
-        scatter(slot, "wait_send")
-        swap(slot, "wait_send")
-        gather(slot, "wait_send")
+    with scope("sends"):
+        for slot in range(3):
+            out_way(slot, "wait_send")
+            back_way(slot, "wait_send")
+        for slot in range(2):
+            scatter(slot, "wait_send")
+            swap(slot, "wait_send")
+            gather(slot, "wait_send")
 
 
 def finish_kernel(*refs):
@@ -565,11 +612,12 @@
     outer = devices // inner
     rows = depth // inner
     tables = transform_tables(seq_length)
-    count = seq_length // LANES * GROUP
+    pieces = width // LANES
+    outer_len = seq_length // LANES
     tables = [jnp.asarray(t) for t in tables]
     hbm = pl.BlockSpec(memory_space=pltpu.HBM)
     vmem = pl.BlockSpec(memory_space=pltpu.VMEM)
-    f32, bf16 = jnp.float32, jnp.bfloat16
+    f32 = jnp.float32
     outs = (
         jax.ShapeDtypeStruct((half, width), f32),
         jax.ShapeDtypeStruct((half, width), f32),
@@ -587,16 +635,13 @@
             pltpu.VMEM((depth, half), f32),
             pltpu.VMEM((half, width), f32),
             *(pltpu.VMEM(t.shape, t.dtype) for t in tables),
-            pltpu.VMEM((2 * count, count), bf16),
-            pltpu.VMEM((2 * count, count), bf16),
-            pltpu.VMEM((count, 2 * count), bf16),
-            pltpu.VMEM((count, 2 * count), bf16),
             pltpu.VMEM((half, width), f32),
-            pltpu.VMEM((2, half, width), f32),
-            pltpu.VMEM((3, devices, GROUP, width), f32),
-            pltpu.VMEM((3, count, 2 * LANES), f32),
-            pltpu.VMEM((3, devices, GROUP, width), f32),
-            pltpu.VMEM((3, half, width), f32),
+            pltpu.VMEM((pieces, half, LANES), f32),
+            pltpu.VMEM((2, pieces, half, LANES), f32),
+            pltpu.VMEM((3, outer_len, GROUP, LANES), f32),
+            pltpu.VMEM((3, outer_len * GROUP, 2 * LANES), f32),
+            pltpu.VMEM((3, outer_len, GROUP, LANES), f32),
+            pltpu.VMEM((3, pieces, half, LANES), f32),
             pltpu.VMEM((2, depth, half), f32),
             pltpu.VMEM((2, inner, rows, half), f32),
             pltpu.VMEM((2, outer, rows, half), f32),
@@ -607,7 +652,7 @@
             pltpu.SemaphoreType.DMA((12,)),
             pltpu.SemaphoreType.DMA((2,)),
             pltpu.SemaphoreType.DMA((2,)),
-            pltpu.SemaphoreType.DMA((5 + len(tables),)),
+            pltpu.SemaphoreType.DMA((4 + pieces + len(tables),)),
         ],
         compiler_params=pltpu.CompilerParams(
             collective_id=0, has_side_effects=True, vmem_limit_bytes=60 * 1024 * 1024
@@ -634,6 +679,7 @@
         and width % LANES == 0
         and channel_count % LANES == 0
         and devices & (devices - 1) == 0
+        and (width * devices // LANES) % 16 == 0
         and value_weight.shape[0] % (GROUP * devices) == 0
     )
     body = fused_device if fits else per_device

time: 55.6 us -> 54.2 us (0.975)
  Pallas kernels: 54.8 us -> 53.4 us
    pallas_call x1, Pallas kernels: 53.8 us -> 52.5 us  [fused_device(): pl.pallas_call(functools.partial(fused_kernel, devices, 1.0 / math.sqrt(s...]
where the time goes in v2:
time: 54.2 us; the launch traced here: 54 us
  Pallas kernels  53.4 us (99%)
  between operations  0.64 us (1%)
    pallas_call x1, Pallas kernels, fused_device(): pl.pallas_call(functools.partial(fused_kernel, devices, 1.0 / math.sqrt(s...  52.5 us

profile of v2, /device:TPU:0, one launch (start us, length us, event | category | flops | bytes accessed | tf_op | source)
XLA Modules:
  0.0 54.0 jit_solution(11544436419572221072)
XLA Ops:
  0.6 52.5 %shard_map.129 = (f32[128,512]{1,0:T(8,128)S(1)}, f32[128,512]{1,0:T(8,128)S(1)}, f32[256,128]{1,0:T(8,128)S(1)}, f32[256,128]{1,0:T(8,128)S(1)}) custom-call(f32[128,512]{1,0:T(8,128)} %refs_0_.1, f32[256,128]{1,0:T(8,128)} %refs_1_.1, f32[256,128]{1,0:T(8,128)} %refs_2_.1, f32[128,512]{1,0:T(8,128)} %refs_3_.1, f32[128,512]{1,0:T(8,128)} %refs_4_.1, ...), custom_call_target="tpu_custom_call" | custom-call | tf_op jit(solution)/shard_map/pallas_call | solution.py:627
  53.1 0.9 %shard_map.130 = (f32[128,512]{1,0:T(8,128)}, f32[128,512]{1,0:T(8,128)}, f32[256,128]{1,0:T(8,128)}, f32[256,128]{1,0:T(8,128)}) custom-call(f32[128,512]{1,0:T(8,128)S(1)} %get-tuple-element.8.refs_0_, f32[128,512]{1,0:T(8,128)S(1)} %get-tuple-element.9.refs_1_, f32[256,128]{1,0:T(8,128)S(1)} %get-tuple-element.10.refs_2_, ...), custom_call_target="tpu_custom_call" | custom-call | tf_op jit(solution)/shard_map/pallas_call | solution.py:662

commit v3 on v2

--- a/solution.py
+++ b/solution.py
@@ -271,7 +271,7 @@
     chan = lax.axis_index("chan")
     half, width = x_ref.shape
     pieces = width // LANES
-    inner = 1 << (devices.bit_length() - 1) // 2
+    inner = devices // 2
     outer = devices // inner
     rows = 2 * half // inner
     me_inner, me_outer = me % inner, me // inner
@@ -335,9 +335,9 @@
             device_id_type=pl.DeviceIdType.MESH,
         )
 
-    def send_each(slot, src_of, dst, count=devices, stride=1):
+    def send_each(slot, src_of, dst, count=devices, stride=1, first=1):
         def step(i, carry):
-            peer = peer_of((count - i) * stride)
+            peer = peer_of((count - 1 - i) * stride)
             pltpu.make_async_remote_copy(
                 src_ref=src_of(peer),
                 dst_ref=dst,
@@ -348,7 +348,7 @@
             ).start()
             return carry
 
-        lax.fori_loop(1, count, step, 0)
+        lax.fori_loop(0, count - first, step, 0)
 
     def drain(slot, ref, what):
         copy = pltpu.make_async_remote_copy(
@@ -376,13 +376,18 @@
         else:
             drain(slot, in_sig.at[slot, pl.ds(0, (devices - 1) * pieces)], what)
 
-    def back_way(slot, what):
+    def back_way(slot, what, first=1, count=devices):
         if what == "start":
             send_each(
                 3 + slot,
                 lambda p: out_sig.at[slot, group_rows(p, pieces)],
                 ret_sig.at[slot, :, group_rows(me, GROUP), :],
+                count,
+                1,
+                first,
             )
+            if first > 1:
+                return
             ret_sig[slot, :, group_rows(me, GROUP), :] = out_sig[slot, group_rows(me, pieces)]
         else:
             drain(3 + slot, out_sig.at[slot, pl.ds(0, (devices - 1) * pieces)], what)
@@ -503,7 +508,6 @@
                 signal = signal * scale
             for at in range(2):
                 target[channel_of(pair + at), :] = signal[:, lanes(at)]
-        back_way(slot, "start")
 
     def returned(slot):
         return jnp.concatenate([ret_sig[slot, piece] for piece in range(pieces)], axis=1)
@@ -518,12 +522,14 @@
         transform(1)
     with scope("r0"):
         restore(0, 1, False, 0)
+        back_way(0, "start")
     with scope("wait2"):
         out_way(2, "wait_recv")
     with scope("t2"):
         transform(2)
     with scope("r1"):
         restore(0, 2, True, 1)
+        back_way(1, "start")
     with scope("r2"):
         restore(1, 2, True, 2)
 
@@ -539,6 +545,11 @@
         back_way(0, "wait_recv")
     grad_query = split(g_ref[...] * returned(0))
     weight_part(0, grad_query)
+
+    @pl.when(chan == 0)
+    def _():
+        back_way(2, "start", 12, 16)
+
     near_grad = dot3(split(qw_ref[own_rows, :]), grad_query)
     far_grad = dot3(split(qw_ref[other_rows, :]), grad_query)
 
@@ -560,15 +571,21 @@
         gath[slot, group_rows(me_inner, rows), :] = total * scale
         gather(slot, "start")
 
-    reduce_inner(0)
     with scope("back1"):
         back_way(1, "wait_recv")
     grad_value = split(returned(1))
     weight_part(1, grad_value)
+
+    @pl.when(chan == 1)
+    def _():
+        back_way(2, "start", 12, 16)
+
     ig_send[...] = far_grad + dot3(split(vw_ref[other_rows, :]), grad_value)
     give_ig = exchange(1, ig_send, ig_recv)
     give_ig.start()
+    reduce_inner(0)
     reduce_inner(1)
+    back_way(2, "start", 1, 12)
     near_grad = near_grad + dot3(split(vw_ref[own_rows, :]), grad_value)
     reduce_outer(0)
     with scope("give_ig"):
@@ -608,7 +625,7 @@
     devices = lax.axis_size("seq")
     seq_length = width * devices
     depth = value_weight.shape[0]
-    inner = 1 << (devices.bit_length() - 1) // 2
+    inner = devices // 2
     outer = devices // inner
     rows = depth // inner
     tables = transform_tables(seq_length)

time: 54.2 us -> 50.9 us (0.939)
  Pallas kernels: 53.4 us -> 50.1 us
    pallas_call x1, Pallas kernels: 52.5 us -> 49.2 us  [fused_device(): pl.pallas_call(functools.partial(fused_kernel, devices, 1.0 / math.sqrt(s...]
where the time goes in v3:
time: 50.9 us; the launch traced here: 50.8 us
  Pallas kernels  50.1 us (98%)
  between operations  0.64 us (1%)
    pallas_call x1, Pallas kernels, fused_device(): pl.pallas_call(functools.partial(fused_kernel, devices, 1.0 / math.sqrt(s...  49.2 us

profile of v3, /device:TPU:0, one launch (start us, length us, event | category | flops | bytes accessed | tf_op | source)
XLA Modules:
  0.0 50.8 jit_solution(1144970877946470018)
XLA Ops:
  0.6 49.2 %shard_map.129 = (f32[128,512]{1,0:T(8,128)S(1)}, f32[128,512]{1,0:T(8,128)S(1)}, f32[256,128]{1,0:T(8,128)S(1)}, f32[256,128]{1,0:T(8,128)S(1)}) custom-call(f32[128,512]{1,0:T(8,128)} %refs_0_.1, f32[256,128]{1,0:T(8,128)} %refs_1_.1, f32[256,128]{1,0:T(8,128)} %refs_2_.1, f32[128,512]{1,0:T(8,128)} %refs_3_.1, f32[128,512]{1,0:T(8,128)} %refs_4_.1, ...), custom_call_target="tpu_custom_call" | custom-call | tf_op jit(solution)/shard_map/pallas_call | solution.py:644
  49.9 0.9 %shard_map.130 = (f32[128,512]{1,0:T(8,128)}, f32[128,512]{1,0:T(8,128)}, f32[256,128]{1,0:T(8,128)}, f32[256,128]{1,0:T(8,128)}) custom-call(f32[128,512]{1,0:T(8,128)S(1)} %get-tuple-element.8.refs_0_, f32[128,512]{1,0:T(8,128)S(1)} %get-tuple-element.9.refs_1_, f32[256,128]{1,0:T(8,128)S(1)} %get-tuple-element.10.refs_2_, ...), custom_call_target="tpu_custom_call" | custom-call | tf_op jit(solution)/shard_map/pallas_call | solution.py:679

commit v4 on v3

--- a/solution.py
+++ b/solution.py
@@ -224,9 +224,12 @@
     c, s = np.cos(inner), np.sin(inner)
     ahead_h, ahead_l = split_table(np.block([[c, -s], [s, c]]).astype(np.float32))
     back_h, back_l = split_table(np.block([[c, s], [-s, c]]).astype(np.float32))
+    first = slice(0, outer // 2)
     return (
         np.concatenate([wide_h, wide_l, wide_h, wide_l], axis=1),
         np.concatenate([tall_h, tall_l, tall_h, tall_l], axis=1),
+        np.concatenate([t[:, first] for t in (wide_h, wide_l, wide_h, wide_l)], axis=1),
+        np.concatenate([t[first] for t in (tall_h, tall_l, tall_h, tall_l)], axis=1),
         np.concatenate([ahead_h, ahead_h, ahead_l], axis=0),
         np.concatenate([back_h, back_h, back_l], axis=0),
         turn,
@@ -261,12 +264,14 @@
 
 def fused_kernel(devices, scale, *refs):
     x_hbm, vw_hbm, qw_hbm, f_hbm, g_hbm = refs[:5]
-    table_hbm = refs[5:10]
-    ig_out, fg_out, vg_out, qg_out = refs[10:14]
-    x_ref, vw_ref, qw_ref, g_ref = refs[14:18]
-    wide_ref, tall_ref, ahead_ref, back_ref, turn_ref = refs[18:23]
-    other_x, f_sig, send_sig, in_sig, spec, out_sig, ret_sig, part, scat, red, gath = refs[23:34]
-    ig_send, ig_recv, ssem, rsem, csend, crecv, lsem = refs[34:]
+    table_hbm = refs[5:12]
+    ig_out, fg_out, vg_out, qg_out = refs[12:16]
+    x_ref, vw_ref, qw_ref, g_ref = refs[16:20]
+    table_refs = refs[20:27]
+    wide_ref, tall_ref, wide_loc_ref, tall_loc_ref, ahead_ref, back_ref, turn_ref = table_refs
+    other_x, f_sig, send_sig, in_sig, spec, out_sig, ret_sig, part, scat, red, gath = refs[27:38]
+    loc_sig, loc_spec, loc_out, loc_ret, ig_send, ig_recv = refs[38:44]
+    ssem, rsem, csend, crecv, lsem = refs[44:]
     me = lax.axis_index("seq")
     chan = lax.axis_index("chan")
     half, width = x_ref.shape
@@ -275,26 +280,27 @@
     outer = devices // inner
     rows = 2 * half // inner
     me_inner, me_outer = me % inner, me // inner
+    near = devices // 2
+    low = me < near
+    high = me >= near
+
+    steps = []
+    while 1 << len(steps) < devices:
+        bit = 1 << len(steps)
+        steps.append((1 - 2 * (me // bit % 2)) * bit)
 
     def peer_of(i):
-        peer, bit = me, 1
-        while bit < devices:
-            peer = peer + (i // bit) % 2 * (1 - 2 * (me // bit % 2)) * bit
-            bit *= 2
-        return peer
+        return me + sum(step for at, step in enumerate(steps) if i >> at & 1)
 
     barrier = pltpu.get_barrier_semaphore()
 
-    def greet(i, carry):
+    for index in reversed(range(1, devices)):
         pl.semaphore_signal(
             barrier,
             inc=1,
-            device_id={"seq": peer_of(devices - i)},
+            device_id={"seq": peer_of(index)},
             device_id_type=pl.DeviceIdType.MESH,
         )
-        return carry
-
-    lax.fori_loop(1, devices, greet, 0)
     pl.semaphore_signal(
         barrier, inc=1, device_id={"chan": 1 - chan}, device_id_type=pl.DeviceIdType.MESH
     )
@@ -306,12 +312,15 @@
         pltpu.make_async_copy(src, dst, lsem.at[at])
         for at, (src, dst) in enumerate(
             [
-                *((f_hbm.at[:, lanes(piece)], f_sig.at[piece]) for piece in range(pieces)),
+                *(
+                    (f_hbm.at[:, :, lanes(piece)], f_sig.at[:, piece])
+                    for piece in range(pieces)
+                ),
                 (x_hbm, x_ref),
                 (vw_hbm, vw_ref),
                 (qw_hbm, qw_ref),
                 (g_hbm, g_ref),
-                *zip(table_hbm, (wide_ref, tall_ref, ahead_ref, back_ref, turn_ref)),
+                *zip(table_hbm, table_refs),
             ]
         )
     ]
@@ -322,6 +331,10 @@
         for load in loads[:count]:
             load.wait()
         del loads[:count]
+
+    @pl.when(high)
+    def _():
+        in_sig[2, : near * pieces] = jnp.zeros_like(in_sig[2, : near * pieces])
 
     pl.semaphore_wait(barrier, devices)
 
@@ -336,8 +349,8 @@
         )
 
     def send_each(slot, src_of, dst, count=devices, stride=1, first=1):
-        def step(i, carry):
-            peer = peer_of((count - 1 - i) * stride)
+        for index in reversed(range(first, count)):
+            peer = peer_of(index * stride)
             pltpu.make_async_remote_copy(
                 src_ref=src_of(peer),
                 dst_ref=dst,
@@ -346,9 +359,6 @@
                 device_id={"seq": peer},
                 device_id_type=pl.DeviceIdType.MESH,
             ).start()
-            return carry
-
-        lax.fori_loop(0, count - first, step, 0)
 
     def drain(slot, ref, what):
         copy = pltpu.make_async_remote_copy(
@@ -364,33 +374,77 @@
     def group_rows(peer, count):
         return pl.ds(pl.multiple_of(peer * count, count), count)
 
+    def messages(slot, count, what):
+        drain(slot, in_sig.at[0, pl.ds(0, count * pieces)], what)
+
+    def split_messages(slot, few, what):
+        @pl.when(few)
+        def _():
+            messages(slot, near - 1, what)
+
+        @pl.when(jnp.logical_not(few))
+        def _():
+            messages(slot, devices - 1, what)
+
     def out_way(slot, what):
+        src = f_sig if slot == 0 else send_sig.at[slot - 1]
+        mine = in_sig.at[slot, group_rows(me, pieces)]
         if what == "start":
-            src = f_sig if slot == 0 else send_sig.at[slot - 1]
-            send_each(
-                slot,
-                lambda p: src.at[:, group_rows(p, GROUP), :],
-                in_sig.at[slot, group_rows(me, pieces)],
-            )
-            in_sig[slot, group_rows(me, pieces)] = src[:, group_rows(me, GROUP), :]
+            if slot < 2:
+                send_each(slot, lambda p: src.at[p], mine, devices, 1, near)
+            else:
+
+                @pl.when(high)
+                def _():
+                    send_each(slot, lambda p: src.at[p], mine, devices, 1, near)
+
+            send_each(slot, lambda p: src.at[p], mine, near)
+            in_sig[slot, group_rows(me, pieces)] = src[me]
+
+            @pl.when(low)
+            def _():
+                own = group_rows(me, pieces)
+                send_each(12 + slot, lambda p: src.at[p + near], loc_sig.at[slot, own], near)
+                loc_sig[slot, own] = src[me + near]
+
+        elif slot < 2:
+            messages(slot, devices - 1, what)
         else:
-            drain(slot, in_sig.at[slot, pl.ds(0, (devices - 1) * pieces)], what)
-
-    def back_way(slot, what, first=1, count=devices):
-        if what == "start":
+            split_messages(slot, high if what == "wait_recv" else low, what)
+
+    def back_way(slot, what):
+        def send(count, first):
             send_each(
                 3 + slot,
                 lambda p: out_sig.at[slot, group_rows(p, pieces)],
-                ret_sig.at[slot, :, group_rows(me, GROUP), :],
+                ret_sig.at[slot, me],
                 count,
                 1,
                 first,
             )
-            if first > 1:
-                return
-            ret_sig[slot, :, group_rows(me, GROUP), :] = out_sig[slot, group_rows(me, pieces)]
+
+        if what == "start":
+            if slot > 0:
+                send(devices, near)
+            else:
+
+                @pl.when(low)
+                def _():
+                    send(devices, near)
+
+            send(near, 1)
+            ret_sig[slot, me] = out_sig[slot, group_rows(me, pieces)]
+        elif slot > 0:
+            messages(3 + slot, devices - 1, what)
         else:
-            drain(3 + slot, out_sig.at[slot, pl.ds(0, (devices - 1) * pieces)], what)
+            split_messages(3, low if what == "wait_recv" else high, what)
+
+    def back_local(slot):
+        own = ret_sig.at[0, me + near] if slot == 0 else loc_ret.at[slot - 1, me]
+        send_each(
+            15 + slot, lambda p: loc_out.at[slot, group_rows(p, pieces)], own, near
+        )
+        own[...] = loc_out[slot, group_rows(me, pieces)]
 
     def scatter(slot, what):
         if what == "start":
@@ -440,7 +494,7 @@
 
     def stage(slot, value):
         for piece in range(pieces):
-            send_sig[slot - 1, piece] = value[:, lanes(piece)]
+            send_sig[slot - 1, :, piece] = value[:, lanes(piece)].reshape(devices, GROUP, LANES)
         with scope("out"):
             out_way(slot, "start")
 
@@ -462,17 +516,19 @@
     def channel_rows(channel):
         return slice(channel * outer_len, (channel + 1) * outer_len)
 
-    def channel_of(channel):
-        return pl.ds(channel, outer_len, stride=GROUP)
-
-    def transform(slot):
-        signal = in_sig.at[slot].reshape(outer_len * GROUP, LANES)
+    def transform(source, table, target):
+        count = source.shape[0]
+        signal = source.reshape(count * GROUP, LANES)
         rows_of = []
         for pair in range(0, GROUP, 2):
             columns = jnp.concatenate(
-                [signal[channel_of(channel), :] for channel in (pair, pair + 1)], axis=1
+                [
+                    signal[pl.ds(channel, count, stride=GROUP), :]
+                    for channel in (pair, pair + 1)
+                ],
+                axis=1,
             )
-            first = dot(wide, right4(columns))
+            first = dot(table, right4(columns))
             for at in range(2):
                 real = first[:outer_len, lanes(at)]
                 imag = first[outer_len:, lanes(at)]
@@ -481,18 +537,19 @@
                         [real * cosine + imag * sine, imag * cosine - real * sine], axis=1
                     )
                 )
-        spec[slot] = dot(left3(jnp.concatenate(rows_of, axis=0)), ahead)
-
-    def restore(first, second, conjugate, slot):
-        real_a, imag_a = spec[first, :, :LANES], spec[first, :, LANES:]
-        real_b, imag_b = spec[second, :, :LANES], spec[second, :, LANES:]
+        target[...] = dot(left3(jnp.concatenate(rows_of, axis=0)), ahead)
+
+    def restore(first, second, conjugate, table, target, factor=None):
+        count = target.shape[0]
+        real_a, imag_a = first[:, :LANES], first[:, LANES:]
+        real_b, imag_b = second[:, :LANES], second[:, LANES:]
         if conjugate:
             imag_a = -imag_a
         product = jnp.concatenate(
             [real_a * real_b - imag_a * imag_b, real_a * imag_b + imag_a * real_b], axis=1
         )
         inverse = dot(left3(product), back)
-        target = out_sig.at[slot].reshape(outer_len * GROUP, LANES)
+        result = target.reshape(count * GROUP, LANES)
         for pair in range(0, GROUP, 2):
             columns = []
             for channel in (pair, pair + 1):
@@ -503,35 +560,81 @@
                         [real * cosine - imag * sine, imag * cosine + real * sine], axis=0
                     )
                 )
-            signal = dot(tall, right4(jnp.concatenate(columns, axis=1)))
-            if slot == 2:
-                signal = signal * scale
+            signal = dot(table, right4(jnp.concatenate(columns, axis=1)))
+            if factor is not None:
+                signal = signal * factor
             for at in range(2):
-                target[channel_of(pair + at), :] = signal[:, lanes(at)]
+                result[pl.ds(pair + at, count, stride=GROUP), :] = signal[:, lanes(at)]
 
     def returned(slot):
-        return jnp.concatenate([ret_sig[slot, piece] for piece in range(pieces)], axis=1)
+        return jnp.concatenate(
+            [ret_sig[slot, :, piece].reshape(half, LANES) for piece in range(pieces)], axis=1
+        )
+
+    def local_transform(slot):
+        with scope(f"locw{slot}"):
+            messages(12 + slot, near - 1, "wait_recv")
+        transform(loc_sig.at[slot], wide_loc_ref[...], loc_spec.at[slot])
+
+    def local_restore(first, second, conjugate, slot, factor=None):
+        restore(
+            loc_spec.at[first],
+            loc_spec.at[second],
+            conjugate,
+            tall_loc_ref[...],
+            loc_out.at[slot],
+            factor,
+        )
 
     with scope("wait0"):
         out_way(0, "wait_recv")
     with scope("t0"):
-        transform(0)
+        transform(in_sig.at[0], wide, spec.at[0])
+    @pl.when(low)
+    def _():
+        local_transform(0)
+        local_transform(1)
+        with scope("locr0"):
+            local_restore(0, 1, False, 0)
+        back_local(0)
+
     with scope("wait1"):
         out_way(1, "wait_recv")
     with scope("t1"):
-        transform(1)
+        transform(in_sig.at[1], wide, spec.at[1])
     with scope("r0"):
-        restore(0, 1, False, 0)
+        restore(spec.at[0], spec.at[1], False, tall, out_sig.at[0])
         back_way(0, "start")
+
+    @pl.when(low)
+    def _():
+        local_transform(2)
+        with scope("locr1"):
+            local_restore(0, 2, True, 1)
+        back_local(1)
+        with scope("locr2"):
+            local_restore(1, 2, True, 2, scale)
+
     with scope("wait2"):
         out_way(2, "wait_recv")
     with scope("t2"):
-        transform(2)
+        transform(in_sig.at[2], wide, spec.at[2])
     with scope("r1"):
-        restore(0, 2, True, 1)
+        restore(spec.at[0], spec.at[2], True, tall, out_sig.at[1])
         back_way(1, "start")
+
     with scope("r2"):
-        restore(1, 2, True, 2)
+        restore(spec.at[1], spec.at[2], True, tall, out_sig.at[2], scale)
+
+    def back_ready(slot):
+        with scope(f"back{slot}"):
+            back_way(slot, "wait_recv")
+
+            @pl.when(low)
+            def _():
+                messages(15 + slot, near - 1, "wait_recv")
+                if slot > 0:
+                    ret_sig[slot, near:] = ret_sig[slot, near:] + loc_ret[slot - 1]
 
     def weight_part(slot, grad):
         part[slot, own_rows, :] = dot3(own_x2, grad, NT)
@@ -541,14 +644,13 @@
 
     own_x2 = split(x_ref[...])
     far_x2 = split(other_x[...])
-    with scope("back0"):
-        back_way(0, "wait_recv")
+    back_ready(0)
     grad_query = split(g_ref[...] * returned(0))
     weight_part(0, grad_query)
 
-    @pl.when(chan == 0)
+    @pl.when(high)
     def _():
-        back_way(2, "start", 12, 16)
+        back_way(2, "start")
 
     near_grad = dot3(split(qw_ref[own_rows, :]), grad_query)
     far_grad = dot3(split(qw_ref[other_rows, :]), grad_query)
@@ -571,29 +673,27 @@
         gath[slot, group_rows(me_inner, rows), :] = total * scale
         gather(slot, "start")
 
-    with scope("back1"):
-        back_way(1, "wait_recv")
+    back_ready(1)
     grad_value = split(returned(1))
     weight_part(1, grad_value)
-
-    @pl.when(chan == 1)
-    def _():
-        back_way(2, "start", 12, 16)
-
     ig_send[...] = far_grad + dot3(split(vw_ref[other_rows, :]), grad_value)
     give_ig = exchange(1, ig_send, ig_recv)
     give_ig.start()
     reduce_inner(0)
     reduce_inner(1)
-    back_way(2, "start", 1, 12)
+
+    @pl.when(low)
+    def _():
+        back_way(2, "start")
+        back_local(2)
+
     near_grad = near_grad + dot3(split(vw_ref[own_rows, :]), grad_value)
     reduce_outer(0)
     with scope("give_ig"):
         give_ig.wait()
     ig_out[...] = near_grad + ig_recv[...]
     reduce_outer(1)
-    with scope("back2"):
-        back_way(2, "wait_recv")
+    back_ready(2)
     fg_out[...] = returned(2)
     for slot, out in ((0, qg_out), (1, vg_out)):
         with scope(f"gather{slot}"):
@@ -607,6 +707,11 @@
             scatter(slot, "wait_send")
             swap(slot, "wait_send")
             gather(slot, "wait_send")
+
+        @pl.when(low)
+        def _():
+            for slot in range(12, 18):
+                messages(slot, near - 1, "wait_send")
 
 
 def finish_kernel(*refs):
@@ -653,20 +758,24 @@
             pltpu.VMEM((half, width), f32),
             *(pltpu.VMEM(t.shape, t.dtype) for t in tables),
             pltpu.VMEM((half, width), f32),
-            pltpu.VMEM((pieces, half, LANES), f32),
-            pltpu.VMEM((2, pieces, half, LANES), f32),
+            pltpu.VMEM((devices, pieces, GROUP, LANES), f32),
+            pltpu.VMEM((2, devices, pieces, GROUP, LANES), f32),
             pltpu.VMEM((3, outer_len, GROUP, LANES), f32),
             pltpu.VMEM((3, outer_len * GROUP, 2 * LANES), f32),
             pltpu.VMEM((3, outer_len, GROUP, LANES), f32),
-            pltpu.VMEM((3, pieces, half, LANES), f32),
+            pltpu.VMEM((3, devices, pieces, GROUP, LANES), f32),
             pltpu.VMEM((2, depth, half), f32),
             pltpu.VMEM((2, inner, rows, half), f32),
             pltpu.VMEM((2, outer, rows, half), f32),
             pltpu.VMEM((2, depth, half), f32),
+            pltpu.VMEM((3, outer_len // 2, GROUP, LANES), f32),
+            pltpu.VMEM((3, outer_len * GROUP, 2 * LANES), f32),
+            pltpu.VMEM((3, outer_len // 2, GROUP, LANES), f32),
+            pltpu.VMEM((2, devices // 2, pieces, GROUP, LANES), f32),
             pltpu.VMEM((half, width), f32),
             pltpu.VMEM((half, width), f32),
-            pltpu.SemaphoreType.DMA((12,)),
-            pltpu.SemaphoreType.DMA((12,)),
+            pltpu.SemaphoreType.DMA((18,)),
+            pltpu.SemaphoreType.DMA((18,)),
             pltpu.SemaphoreType.DMA((2,)),
             pltpu.SemaphoreType.DMA((2,)),
             pltpu.SemaphoreType.DMA((4 + pieces + len(tables),)),
@@ -674,7 +783,14 @@
         compiler_params=pltpu.CompilerParams(
             collective_id=0, has_side_effects=True, vmem_limit_bytes=60 * 1024 * 1024
         ),
-    )(inputs, value_weight, query_weight, filters, grad_out, *tables)
+    )(
+        inputs,
+        value_weight,
+        query_weight,
+        filters.reshape(devices, GROUP, width),
+        grad_out,
+        *tables,
+    )
     return tuple(
         pl.pallas_call(
             finish_kernel,
@@ -696,7 +812,7 @@
         and width % LANES == 0
         and channel_count % LANES == 0
         and devices & (devices - 1) == 0
-        and (width * devices // LANES) % 16 == 0
+        and (width * devices // LANES) % 32 == 0
         and value_weight.shape[0] % (GROUP * devices) == 0
     )
     body = fused_device if fits else per_device

time: 50.9 us -> 49.9 us (0.980)
  Pallas kernels: 50.1 us -> 49.1 us
    pallas_call x1, Pallas kernels: 49.2 us -> 48.2 us  [fused_device(): pl.pallas_call(functools.partial(fused_kernel, devices, 1.0 / math.sqrt(s...]
where the time goes in v4:
time: 49.9 us; the launch traced here: 49.7 us
  Pallas kernels  49.1 us (98%)
  between operations  0.64 us (1%)
    pallas_call x1, Pallas kernels, fused_device(): pl.pallas_call(functools.partial(fused_kernel, devices, 1.0 / math.sqrt(s...  48.2 us

profile of v4, /device:TPU:0, one launch (start us, length us, event | category | flops | bytes accessed | tf_op | source)
XLA Modules:
  0.0 49.7 jit_solution(425909615468409967)
XLA Ops:
  0.6 48.2 %shard_map.147 = (f32[128,512]{1,0:T(8,128)S(1)}, f32[128,512]{1,0:T(8,128)S(1)}, f32[256,128]{1,0:T(8,128)S(1)}, f32[256,128]{1,0:T(8,128)S(1)}) custom-call(f32[128,512]{1,0:T(8,128)} %refs_0_.1, f32[256,128]{1,0:T(8,128)} %refs_1_.1, f32[256,128]{1,0:T(8,128)} %refs_2_.1, f32[16,8,512]{2,1,0:T(8,128)} %bitcast.1, f32[128,512]{1,0:T(8,128)} %refs_4_.1, ...), custom_call_target="tpu_custom_call" | custom-call | tf_op jit(solution)/shard_map/pallas_call | solution.py:749
  48.8 0.9 %shard_map.148 = (f32[128,512]{1,0:T(8,128)}, f32[128,512]{1,0:T(8,128)}, f32[256,128]{1,0:T(8,128)}, f32[256,128]{1,0:T(8,128)}) custom-call(f32[128,512]{1,0:T(8,128)S(1)} %get-tuple-element.8.refs_0_, f32[128,512]{1,0:T(8,128)S(1)} %get-tuple-element.9.refs_1_, f32[256,128]{1,0:T(8,128)S(1)} %get-tuple-element.10.refs_2_, ...), custom_call_target="tpu_custom_call" | custom-call | tf_op jit(solution)/shard_map/pallas_call | solution.py:795

commit v5 on v4

--- a/solution.py
+++ b/solution.py
@@ -626,6 +626,11 @@
     with scope("r2"):
         restore(spec.at[1], spec.at[2], True, tall, out_sig.at[2], scale)
 
+    @pl.when(high & (chan == 1))
+    def _():
+        back_way(2, "start")
+
+
     def back_ready(slot):
         with scope(f"back{slot}"):
             back_way(slot, "wait_recv")
@@ -648,9 +653,10 @@
     grad_query = split(g_ref[...] * returned(0))
     weight_part(0, grad_query)
 
-    @pl.when(high)
+    @pl.when(high & (chan == 0))
     def _():
         back_way(2, "start")
+
 
     near_grad = dot3(split(qw_ref[own_rows, :]), grad_query)
     far_grad = dot3(split(qw_ref[other_rows, :]), grad_query)
@@ -686,6 +692,7 @@
     def _():
         back_way(2, "start")
         back_local(2)
+
 
     near_grad = near_grad + dot3(split(vw_ref[own_rows, :]), grad_value)
     reduce_outer(0)

time: 49.9 us -> 49.9 us (level)
  no operation moved by 1% of the time
where the time goes in v5:
time: 49.9 us; the launch traced here: 49.7 us
  Pallas kernels  49.1 us (98%)
  between operations  0.64 us (1%)
    pallas_call x1, Pallas kernels, fused_device(): pl.pallas_call(functools.partial(fused_kernel, devices, 1.0 / math.sqrt(s...  48.2 us

profile of v5, /device:TPU:0, one launch (start us, length us, event | category | flops | bytes accessed | tf_op | source)
XLA Modules:
  0.0 49.7 jit_solution(18082006112048033809)
XLA Ops:
  0.6 48.2 %shard_map.147 = (f32[128,512]{1,0:T(8,128)S(1)}, f32[128,512]{1,0:T(8,128)S(1)}, f32[256,128]{1,0:T(8,128)S(1)}, f32[256,128]{1,0:T(8,128)S(1)}) custom-call(f32[128,512]{1,0:T(8,128)} %refs_0_.1, f32[256,128]{1,0:T(8,128)} %refs_1_.1, f32[256,128]{1,0:T(8,128)} %refs_2_.1, f32[16,8,512]{2,1,0:T(8,128)} %bitcast.1, f32[128,512]{1,0:T(8,128)} %refs_4_.1, ...), custom_call_target="tpu_custom_call" | custom-call | tf_op jit(solution)/shard_map/pallas_call | solution.py:756
  48.8 0.9 %shard_map.148 = (f32[128,512]{1,0:T(8,128)}, f32[128,512]{1,0:T(8,128)}, f32[256,128]{1,0:T(8,128)}, f32[256,128]{1,0:T(8,128)}) custom-call(f32[128,512]{1,0:T(8,128)S(1)} %get-tuple-element.8.refs_0_, f32[128,512]{1,0:T(8,128)S(1)} %get-tuple-element.9.refs_1_, f32[256,128]{1,0:T(8,128)S(1)} %get-tuple-element.10.refs_2_, ...), custom_call_target="tpu_custom_call" | custom-call | tf_op jit(solution)/shard_map/pallas_call | solution.py:802

commit v6 on v4

--- a/solution.py
+++ b/solution.py
@@ -309,7 +309,7 @@
         return slice(piece * LANES, (piece + 1) * LANES)
 
     loads = [
-        pltpu.make_async_copy(src, dst, lsem.at[at])
+        pltpu.make_async_copy(src, dst, lsem.at[max(at - pieces + 1, 0)])
         for at, (src, dst) in enumerate(
             [
                 *(
@@ -479,7 +479,8 @@
     give_x = exchange(0, x_hbm, other_x)
     give_x.start()
     with scope("load_f"):
-        wait_loads(pieces)
+        pltpu.make_async_copy(f_sig, f_sig, lsem.at[0]).wait()
+        del loads[:pieces]
     with scope("out0"):
         out_way(0, "start")
 
@@ -778,7 +779,7 @@
             pltpu.SemaphoreType.DMA((18,)),
             pltpu.SemaphoreType.DMA((2,)),
             pltpu.SemaphoreType.DMA((2,)),
-            pltpu.SemaphoreType.DMA((4 + pieces + len(tables),)),
+            pltpu.SemaphoreType.DMA((5 + len(tables),)),
         ],
         compiler_params=pltpu.CompilerParams(
             collective_id=0, has_side_effects=True, vmem_limit_bytes=60 * 1024 * 1024

time: 49.9 us -> 49.8 us (level)
  no operation moved by 1% of the time
where the time goes in v6:
time: 49.8 us; the launch traced here: 49.7 us
  Pallas kernels  49.1 us (99%)
  between operations  0.64 us (1%)
    pallas_call x1, Pallas kernels, fused_device(): pl.pallas_call(functools.partial(fused_kernel, devices, 1.0 / math.sqrt(s...  48.1 us

profile of v6, /device:TPU:0, one launch (start us, length us, event | category | flops | bytes accessed | tf_op | source)
XLA Modules:
  0.0 49.7 jit_solution(8612321918978127968)
XLA Ops:
  0.6 48.1 %shard_map.147 = (f32[128,512]{1,0:T(8,128)S(1)}, f32[128,512]{1,0:T(8,128)S(1)}, f32[256,128]{1,0:T(8,128)S(1)}, f32[256,128]{1,0:T(8,128)S(1)}) custom-call(f32[128,512]{1,0:T(8,128)} %refs_0_.1, f32[256,128]{1,0:T(8,128)} %refs_1_.1, f32[256,128]{1,0:T(8,128)} %refs_2_.1, f32[16,8,512]{2,1,0:T(8,128)} %bitcast.1, f32[128,512]{1,0:T(8,128)} %refs_4_.1, ...), custom_call_target="tpu_custom_call" | custom-call | tf_op jit(solution)/shard_map/pallas_call | solution.py:750
  48.8 0.9 %shard_map.148 = (f32[128,512]{1,0:T(8,128)}, f32[128,512]{1,0:T(8,128)}, f32[256,128]{1,0:T(8,128)}, f32[256,128]{1,0:T(8,128)}) custom-call(f32[128,512]{1,0:T(8,128)S(1)} %get-tuple-element.8.refs_0_, f32[128,512]{1,0:T(8,128)S(1)} %get-tuple-element.9.refs_1_, f32[256,128]{1,0:T(8,128)S(1)} %get-tuple-element.10.refs_2_, ...), custom_call_target="tpu_custom_call" | custom-call | tf_op jit(solution)/shard_map/pallas_call | solution.py:796
